TPU v7x, 32 devices: a whole 2x2x4 slice. The times are simulated.
32 devices in a mesh: groups: 2 (over x), seq: 16 (over z, y, core).
Axes of the slice: x: 2, y: 2, z: 4, core: 2. Of those that a mesh axis runs over, the one named last changes fastest.
Arguments:
- queries: bfloat16 [32, 384, 1280], P(('groups', 'seq')), parts along dimension 0, may hold values from -11 to 11
- key_vectors: bfloat16 [32, 384, 1280], P(('groups', 'seq')), parts along dimension 0, may hold values from -11 to 11
- value_vectors: bfloat16 [32, 384, 1280], P(('groups', 'seq')), parts along dimension 0, may hold values from -5 to 5
- out_grad: bfloat16 [32, 384, 1280], P(('groups', 'seq')), parts along dimension 0, may hold values from -5 to 5
- tile_lists: int32 [16, 5], P('groups'), parts along dimension 0, may hold values from -1 to 7, as said below
Outputs:
- attended: bfloat16 [32, 384, 1280], P(('groups', 'seq')), parts along dimension 0
- query_grad: bfloat16 [32, 384, 1280], P(('groups', 'seq')), parts along dimension 0
- key_grad: bfloat16 [32, 384, 1280], P(('groups', 'seq')), parts along dimension 0
- value_grad: bfloat16 [32, 384, 1280], P(('groups', 'seq')), parts along dimension 0
There are 2 independent parts, one for each index of `groups`. A program takes and returns all parts, laid end to end along the dimension named above; each array names one. Nothing has to cross between parts.
Inputs may be any that keep to these rules, and one draw needn't show every extreme that they name: `tile_lists`: row s lists in ascending order tile s itself, every neighbour of s along the width inside the grid, and some of its neighbours along height and time, then -1 in the unused slots.
All inputs are finite; a program needn't handle non-finite values.
Results may differ from a plain program's by a relative error of at most 0.023.
Values may be sent and summed in bfloat16 or wider, within the bound.
A program may use at most 192 MiB of HBM per device.

v0:
```python
import functools

import jax
import jax.numpy as jnp
from jax import lax
from jax.experimental import pallas as pl
from jax.experimental.pallas import tpu as pltpu
from jax.sharding import PartitionSpec as P

HD = 128
MESH = pl.DeviceIdType.MESH


def dot(a, b, a_dim, b_dim):
    return lax.dot_general(
        a, b, (((a_dim,), (b_dim,)), ((), ())), preferred_element_type=jnp.float32
    )


def neighbours(grid_w):
    tile = lax.axis_index("seq") // 2
    bit0 = lax.rem(tile, 2)
    bit1 = lax.rem(tile // 2, 2)
    column = tile // 4
    if grid_w == 2:
        sides = [(tile + 4 - 8 * column, None, 0)]
    else:
        sides = [(tile - 4, column > 0, 1), (tile + 4, column < grid_w - 1, 0)]
    count = len(sides)
    return sides + [
        (tile + 2 - 4 * bit1, None, count),
        (tile + 1 - 2 * bit0, None, count + 1),
    ]


def when(exists, fn):
    if exists is None:
        fn()
    else:
        pl.when(exists)(fn)


def kernel(
    grid_w, lists_ref, q_ref, k_ref, v_ref, g_ref, o_ref, dq_ref, dk_ref, dv_ref,
    kv_in, probs, term_out, term_in, kv_send, kv_recv, term_send, term_recv,
):
    me = lax.axis_index("seq")
    tile = me // 2
    core = lax.rem(me, 2)
    near = neighbours(grid_w)
    heads = q_ref.shape[2] // HD
    scale = HD ** (-0.5)

    def cols(head):
        return pl.ds(pl.multiple_of(head * HD, HD), HD)

    def kv_copy(slot, there, target, head, kind):
        return pltpu.make_async_remote_copy(
            src_ref=(k_ref, v_ref)[kind].at[0, :, cols(head)],
            dst_ref=kv_in.at[there, head, kind],
            send_sem=kv_send.at[slot, head, kind],
            recv_sem=kv_recv.at[there, head, kind],
            device_id={"seq": target * 2 + core},
            device_id_type=MESH,
        )

    def term_copy(slot, there, target, head):
        return pltpu.make_async_remote_copy(
            src_ref=term_out.at[slot, head],
            dst_ref=term_in.at[there, head],
            send_sem=term_send.at[slot, head],
            recv_sem=term_recv.at[there, head],
            device_id={"seq": target * 2 + core},
            device_id_type=MESH,
        )

    barrier = pltpu.get_barrier_semaphore()
    for target, exists, _ in near:
        when(exists, lambda target=target: pl.semaphore_signal(
            barrier, inc=1, device_id={"seq": target * 2 + core}, device_id_type=MESH))
    pl.semaphore_wait(
        barrier, sum(1 if e is None else jnp.where(e, 1, 0).astype(jnp.int32) for _, e, _ in near)
    )

    @pl.loop(0, heads)
    def _(head):
        for slot, (target, exists, there) in enumerate(near):
            def go(slot=slot, target=target, there=there):
                for kind in range(2):
                    kv_copy(slot, there, target, head, kind).start()
            when(exists, go)

    for slot, (target, exists, there) in enumerate(near):
        if exists is not None:
            @pl.when(jnp.logical_not(exists))
            def _(slot=slot):
                @pl.loop(0, heads)
                def _(head):
                    kv_in[slot, head] = jnp.zeros(kv_in.shape[2:], kv_in.dtype)
                    term_in[slot, head] = jnp.zeros(term_in.shape[2:], term_in.dtype)

    listed = [lists_ref[tile, j] for j in range(lists_ref.shape[1])]

    def bias_of(target, exists):
        found = listed[0] == target
        for entry in listed[1:]:
            found = found | (entry == target)
        if exists is not None:
            found = found & exists
        return jnp.where(found, jnp.float32(0), jnp.float32(-jnp.inf))

    biases = [bias_of(tile, None)] + [bias_of(target, exists) for target, exists, _ in near]

    @pl.loop(0, heads)
    def _(head):
        for slot, (target, exists, _) in enumerate(near):
            def arrived(slot=slot, target=target):
                for kind in range(2):
                    kv_copy(slot, slot, target, head, kind).wait_recv()
            when(exists, arrived)

        here = cols(head)
        query = q_ref[0, :, here]
        grad = g_ref[0, :, here]

        def keys(block):
            return k_ref[0, :, here] if block == 0 else kv_in[block - 1, head, 0]

        def values(block):
            return v_ref[0, :, here] if block == 0 else kv_in[block - 1, head, 1]

        blocks = range(len(near) + 1)
        top = None
        for block in blocks:
            scores = dot(keys(block), query, 1, 1) * scale
            probs[block] = scores
            block_top = jnp.max(scores, axis=0, keepdims=True) + biases[block]
            top = block_top if top is None else jnp.maximum(top, block_top)
        total = jnp.zeros_like(top)
        for block in blocks:
            powers = jnp.exp(probs[block] - (top - biases[block]))
            probs[block] = powers
            total = total + jnp.sum(powers, axis=0, keepdims=True)
        share = 1.0 / total
        mixed = jnp.zeros((HD, query.shape[0]), jnp.float32)
        for block in blocks:
            chance = probs[block] * share
            probs[block] = chance
            mixed = mixed + dot(values(block), chance.astype(jnp.bfloat16), 0, 0)
        mixed = mixed.astype(jnp.bfloat16).astype(jnp.float32)
        o_ref[0, :, here] = mixed.T.astype(jnp.bfloat16)
        delta = jnp.sum(grad.astype(jnp.float32).T * mixed, axis=0, keepdims=True)
        query_sum = jnp.zeros((HD, query.shape[0]), jnp.float32)
        for block in list(blocks)[1:] + [0]:
            chance = probs[block]
            pressure = dot(values(block), grad, 1, 1)
            score_grad = (chance * (pressure - delta)).astype(jnp.bfloat16)
            value_term = dot(chance.astype(jnp.bfloat16), grad, 1, 0).astype(jnp.bfloat16)
            key_term = (scale * dot(score_grad, query, 1, 0)).astype(jnp.bfloat16)
            if block == 0:
                dk_ref[0, :, here] = key_term
                dv_ref[0, :, here] = value_term
            else:
                target, exists, there = near[block - 1]
                term_out[block - 1, head, 0] = key_term
                term_out[block - 1, head, 1] = value_term
                when(exists, lambda: term_copy(block - 1, there, target, head).start())
            query_sum = query_sum + dot(keys(block), score_grad, 0, 0)
        dq_ref[0, :, here] = (scale * query_sum).T.astype(jnp.bfloat16)

    @pl.loop(0, heads)
    def _(head):
        here = cols(head)
        for slot, (target, exists, _) in enumerate(near):
            when(exists, lambda: term_copy(slot, slot, target, head).wait_recv())
        for kind, out in enumerate((dk_ref, dv_ref)):
            sums = out[0, :, here].astype(jnp.float32)
            for slot in range(len(near)):
                sums = sums + term_in[slot, head, kind].astype(jnp.float32)
            out[0, :, here] = sums.astype(jnp.bfloat16)

    @pl.loop(0, heads)
    def _(head):
        for slot, (target, exists, there) in enumerate(near):
            def left(slot=slot, target=target, there=there):
                for kind in range(2):
                    kv_copy(slot, there, target, head, kind).wait_send()
                term_copy(slot, there, target, head).wait_send()
            when(exists, left)


def on_device(queries, key_vectors, value_vectors, out_grad, tile_lists):
    grid_w = lax.axis_size("seq") // 8
    tok, width = queries.shape[1:]
    heads = width // HD
    near = 3 if grid_w == 2 else 4
    vmem = pl.BlockSpec(memory_space=pltpu.VMEM)
    out = jax.ShapeDtypeStruct(queries.shape, jnp.bfloat16)
    slots = pltpu.VMEM((near, heads, 2, tok, HD), jnp.bfloat16)
    dma = pltpu.SemaphoreType.DMA
    return pl.pallas_call(
        functools.partial(kernel, grid_w),
        out_shape=(out,) * 4,
        in_specs=[pl.BlockSpec(memory_space=pltpu.SMEM)] + [vmem] * 4,
        out_specs=(vmem,) * 4,
        scratch_shapes=[
            slots,
            pltpu.VMEM((near + 1, tok, tok), jnp.float32),
            slots,
            slots,
            dma((near, heads, 2)),
            dma((near, heads, 2)),
            dma((near, heads)),
            dma((near, heads)),
        ],
        compiler_params=pltpu.CompilerParams(
            collective_id=0, has_side_effects=True, vmem_limit_bytes=56 * 2**20
        ),
        name="tiles",
    )(tile_lists, queries, key_vectors, value_vectors, out_grad)


def solution(mesh):
    rows = P(("groups", "seq"), None, None)
    return jax.shard_map(
        on_device,
        mesh=mesh,
        in_specs=(rows,) * 4 + (P("groups", None),),
        out_specs=(rows,) * 4,
        check_vma=False,
    )
```

profile of v0, /device:TPU:0, one launch (start us, length us, event | category | flops | bytes accessed | tf_op | source)
XLA Modules:
  0.0 188.3 jit_solution(9058910529731973525)
XLA Ops:
  0.6 181.3 %tiles.1 = (bf16[1,384,1280]{2,1,0:T(8,128)(2,1)}, bf16[1,384,1280]{2,1,0:T(8,128)(2,1)}, bf16[1,384,1280]{2,1,0:T(8,128)(2,1)}, bf16[1,384,1280]{2,1,0:T(8,128)(2,1)}) custom-call(s32[8,5]{1,0:T(8,128)} %lists_ref.1, bf16[1,384,1280]{2,1,0:T(8,128)(2,1)} %q_ref.1, bf16[1,384,1280]{2,1,0:T(8,128)(2,1)} %k_ref.1, bf16[1,384,1280]{2,1,0:T(8,128)(2,1)} %v_ref.1, ...), custom_call_target="tpu_custom_call" | custom-call | tf_op jit(solution)/shard_map/tiles/pallas_call | solution.py:201
  182.0 0.0 copy-start.2
  182.0 2.3 %copy.13 = bf16[1,384,1280]{2,1,0:T(8,128)(2,1)} copy(bf16[1,384,1280]{2,1,0:T(8,128)(2,1)} %get-tuple-element.8) | data formatting | bytes 1966080
  184.3 0.0 copy-done.2
  184.3 0.0 copy-start.1
  184.3 0.9 copy.14
  185.2 0.6 copy-done.1
  185.8 0.0 copy-start
  185.8 0.9 copy.15
  186.8 0.6 copy-done
  187.4 0.9 copy.16
Async XLA Ops:
  182.0 2.3 %copy-start.2 = (bf16[1,384,1280]{2,1,0:T(8,128)(2,1)S(1)}, bf16[1,384,1280]{2,1,0:T(8,128)(2,1)}, u32[]{:S(2)}) copy-start(bf16[1,384,1280]{2,1,0:T(8,128)(2,1)} %get-tuple-element.9) | copy-start | bytes 2949124
  184.3 1.6 copy-start.1
  185.8 1.6 copy-start
where the time goes:
time: 189 us; the launch traced here: 188 us
  Pallas kernels  181 us (96%)
  local copies, waits for them, and re-layouts  6.35 us (3%)
    pallas_call x1, Pallas kernels, on_device(): pl.pallas_call(functools.partial(kernel, grid_w), out_shape=(out,) * 4, i...  181 us
    unnamed x10, local copies, waits for them, and re-layouts  6.35 us

commit v1 on v0

--- a/solution.py
+++ b/solution.py
@@ -41,8 +41,8 @@
 
 
 def kernel(
-    grid_w, lists_ref, q_ref, k_ref, v_ref, g_ref, o_ref, dq_ref, dk_ref, dv_ref,
-    kv_in, probs, term_out, term_in, kv_send, kv_recv, term_send, term_recv,
+    grid_w, lists_ref, q_hbm, k_hbm, v_hbm, g_hbm, o_ref, dq_ref, dk_ref, dv_ref,
+    q_ref, k_ref, v_ref, g_ref, own_sems, kv_in, probs, term_out, term_in, kv_send, kv_recv, term_send, term_recv,
 ):
     me = lax.axis_index("seq")
     tile = me // 2
@@ -56,7 +56,7 @@
 
     def kv_copy(slot, there, target, head, kind):
         return pltpu.make_async_remote_copy(
-            src_ref=(k_ref, v_ref)[kind].at[0, :, cols(head)],
+            src_ref=(k_hbm, v_hbm)[kind].at[0, :, cols(head)],
             dst_ref=kv_in.at[there, head, kind],
             send_sem=kv_send.at[slot, head, kind],
             recv_sem=kv_recv.at[there, head, kind],
@@ -99,6 +99,15 @@
                     kv_in[slot, head] = jnp.zeros(kv_in.shape[2:], kv_in.dtype)
                     term_in[slot, head] = jnp.zeros(term_in.shape[2:], term_in.dtype)
 
+    own = [
+        pltpu.make_async_copy(source, held, own_sems.at[i])
+        for i, (source, held) in enumerate(
+            ((k_hbm, k_ref), (q_hbm, q_ref), (v_hbm, v_ref), (g_hbm, g_ref))
+        )
+    ]
+    for copy in own:
+        copy.start()
+
     listed = [lists_ref[tile, j] for j in range(lists_ref.shape[1])]
 
     def bias_of(target, exists):
@@ -110,6 +119,9 @@
         return jnp.where(found, jnp.float32(0), jnp.float32(-jnp.inf))
 
     biases = [bias_of(tile, None)] + [bias_of(target, exists) for target, exists, _ in near]
+
+    for copy in own:
+        copy.wait()
 
     @pl.loop(0, heads)
     def _(head):
@@ -195,15 +207,18 @@
     heads = width // HD
     near = 3 if grid_w == 2 else 4
     vmem = pl.BlockSpec(memory_space=pltpu.VMEM)
-    out = jax.ShapeDtypeStruct(queries.shape, jnp.bfloat16)
+    out = pltpu.VMEM(queries.shape, jnp.bfloat16)
+    held = pltpu.VMEM(queries.shape, jnp.bfloat16)
+    hbm = pl.BlockSpec(memory_space=pltpu.HBM)
     slots = pltpu.VMEM((near, heads, 2, tok, HD), jnp.bfloat16)
     dma = pltpu.SemaphoreType.DMA
     return pl.pallas_call(
         functools.partial(kernel, grid_w),
         out_shape=(out,) * 4,
-        in_specs=[pl.BlockSpec(memory_space=pltpu.SMEM)] + [vmem] * 4,
+        in_specs=[pl.BlockSpec(memory_space=pltpu.SMEM)] + [hbm] * 4,
         out_specs=(vmem,) * 4,
-        scratch_shapes=[
+        scratch_shapes=[held] * 4 + [
+            dma((4,)),
             slots,
             pltpu.VMEM((near + 1, tok, tok), jnp.float32),
             slots,
@@ -214,7 +229,7 @@
             dma((near, heads)),
         ],
         compiler_params=pltpu.CompilerParams(
-            collective_id=0, has_side_effects=True, vmem_limit_bytes=56 * 2**20
+            collective_id=0, has_side_effects=True, vmem_limit_bytes=50 * 2**20
         ),
         name="tiles",
     )(tile_lists, queries, key_vectors, value_vectors, out_grad)

time: 189 us -> 183 us (0.968)
  Pallas kernels: 181 us -> 178 us
    pallas_call x1, Pallas kernels: 181 us -> 178 us  [on_device(): pl.pallas_call(functools.partial(kernel, grid_w), out_shape=(out,) * 4, i...]
    unnamed x10 -> x6, local copies, waits for them, and re-layouts: 6.35 us -> 4.46 us
where the time goes in v1:
time: 183 us
  Pallas kernels  178 us (97%)
  local copies, waits for them, and re-layouts  4.46 us (2%)
    pallas_call x1, Pallas kernels, on_device(): pl.pallas_call(functools.partial(kernel, grid_w), out_shape=(out,) * 4, i...  178 us
    unnamed x6, local copies, waits for them, and re-layouts  4.46 us

profile of v1, /device:TPU:0, one launch (start us, length us, event | category | flops | bytes accessed | tf_op | source)
XLA Modules:
  0.0 183.2 jit_solution(7256519418279577217)
XLA Ops:
  0.6 0.0 copy-start
  0.6 0.7 copy-done
  1.3 178.1 %tiles.1 = (bf16[1,384,1280]{2,1,0:T(8,128)(2,1)S(1)}, bf16[1,384,1280]{2,1,0:T(8,128)(2,1)S(1)}, bf16[1,384,1280]{2,1,0:T(8,128)(2,1)S(1)}, bf16[1,384,1280]{2,1,0:T(8,128)(2,1)S(1)}) custom-call(s32[8,5]{1,0:T(8,128)S(1)} %copy-done, bf16[1,384,1280]{2,1,0:T(8,128)(2,1)} %q_hbm.1, bf16[1,384,1280]{2,1,0:T(8,128)(2,1)} %k_hbm.1, ...), custom_call_target="tpu_custom_call" | custom-call | tf_op jit(solution)/shard_map/tiles/pallas_call | solution.py:215
  179.5 0.9 copy.13
  180.4 0.9 copy.14
  181.4 0.9 copy.15
  182.3 0.9 copy.16
Async XLA Ops:
  0.6 0.7 copy-start

commit v2 on v1

--- a/solution.py
+++ b/solution.py
@@ -41,8 +41,8 @@
 
 
 def kernel(
-    grid_w, lists_ref, q_hbm, k_hbm, v_hbm, g_hbm, o_ref, dq_ref, dk_ref, dv_ref,
-    q_ref, k_ref, v_ref, g_ref, own_sems, kv_in, probs, term_out, term_in, kv_send, kv_recv, term_send, term_recv,
+    grid_w, lists_hbm, q_hbm, k_hbm, v_hbm, g_hbm, o_ref, dq_ref, dk_ref, dv_ref,
+    lists_ref, q_ref, k_ref, v_ref, g_ref, own_sems, kv_in, probs, term_out, term_in, kv_send, kv_recv, term_send, term_recv,
 ):
     me = lax.axis_index("seq")
     tile = me // 2
@@ -102,11 +102,20 @@
     own = [
         pltpu.make_async_copy(source, held, own_sems.at[i])
         for i, (source, held) in enumerate(
-            ((k_hbm, k_ref), (q_hbm, q_ref), (v_hbm, v_ref), (g_hbm, g_ref))
+            (
+                (lists_hbm, lists_ref),
+                (k_hbm, k_ref),
+                (q_hbm, q_ref),
+                (v_hbm, v_ref),
+                (g_hbm, g_ref),
+            )
         )
     ]
     for copy in own:
         copy.start()
+
+    for copy in own:
+        copy.wait()
 
     listed = [lists_ref[tile, j] for j in range(lists_ref.shape[1])]
 
@@ -119,9 +128,6 @@
         return jnp.where(found, jnp.float32(0), jnp.float32(-jnp.inf))
 
     biases = [bias_of(tile, None)] + [bias_of(target, exists) for target, exists, _ in near]
-
-    for copy in own:
-        copy.wait()
 
     @pl.loop(0, heads)
     def _(head):
@@ -201,6 +207,24 @@
             when(exists, left)
 
 
+def store(*refs):
+    sems = refs[8]
+    rows = refs[0].shape[1] // 2
+    copies = [
+        pltpu.make_async_copy(
+            refs[i].at[:, pl.ds(part * rows, rows)],
+            refs[4 + i].at[:, pl.ds(part * rows, rows)],
+            sems.at[i, part],
+        )
+        for i in range(4)
+        for part in range(2)
+    ]
+    for copy in copies:
+        copy.start()
+    for copy in copies:
+        copy.wait()
+
+
 def on_device(queries, key_vectors, value_vectors, out_grad, tile_lists):
     grid_w = lax.axis_size("seq") // 8
     tok, width = queries.shape[1:]
@@ -212,13 +236,13 @@
     hbm = pl.BlockSpec(memory_space=pltpu.HBM)
     slots = pltpu.VMEM((near, heads, 2, tok, HD), jnp.bfloat16)
     dma = pltpu.SemaphoreType.DMA
-    return pl.pallas_call(
+    results = pl.pallas_call(
         functools.partial(kernel, grid_w),
         out_shape=(out,) * 4,
-        in_specs=[pl.BlockSpec(memory_space=pltpu.SMEM)] + [hbm] * 4,
+        in_specs=[hbm] * 5,
         out_specs=(vmem,) * 4,
-        scratch_shapes=[held] * 4 + [
-            dma((4,)),
+        scratch_shapes=[pltpu.SMEM(tile_lists.shape, jnp.int32)] + [held] * 4 + [
+            dma((5,)),
             slots,
             pltpu.VMEM((near + 1, tok, tok), jnp.float32),
             slots,
@@ -229,10 +253,22 @@
             dma((near, heads)),
         ],
         compiler_params=pltpu.CompilerParams(
-            collective_id=0, has_side_effects=True, vmem_limit_bytes=50 * 2**20
+            collective_id=0, has_side_effects=True, vmem_limit_bytes=42 * 2**20
         ),
         name="tiles",
-    )(tile_lists, queries, key_vectors, value_vectors, out_grad)
+    )(*[
+        pltpu.with_memory_space_constraint(a, pltpu.HBM)
+        for a in (tile_lists, queries, key_vectors, value_vectors, out_grad)
+    ])
+    return pl.pallas_call(
+        store,
+        out_shape=(jax.ShapeDtypeStruct(queries.shape, jnp.bfloat16),) * 4,
+        in_specs=[vmem] * 4,
+        out_specs=(hbm,) * 4,
+        scratch_shapes=[dma((4, 2))],
+        compiler_params=pltpu.CompilerParams(vmem_limit_bytes=8 * 2**20),
+        name="store",
+    )(*[pltpu.with_memory_space_constraint(r, pltpu.VMEM) for r in results])
 
 
 def solution(mesh):

time: 183 us -> 180 us (0.984)
  local copies, waits for them, and re-layouts: 4.46 us -> 0 us
  Pallas kernels: 178 us -> 180 us
    unnamed x6 -> x0, local copies, waits for them, and re-layouts: 4.46 us -> none
    pallas_call x0 -> x1, Pallas kernels: none -> 1.99 us  [on_device(): pl.pallas_call(store, out_shape=(jax.ShapeDtypeStruct(queries.shape, jnp....]
where the time goes in v2:
time: 180 us
  Pallas kernels  180 us (100%)
    pallas_call x1, Pallas kernels, on_device(): pl.pallas_call(functools.partial(kernel, grid_w), out_shape=(out,) * 4, i...  178 us

profile of v2, /device:TPU:0, one launch (start us, length us, event | category | flops | bytes accessed | tf_op | source)
XLA Modules:
  0.0 180.2 jit_solution(247902121600053853)
XLA Ops:
  0.6 177.6 %tiles.1 = (bf16[1,384,1280]{2,1,0:T(8,128)(2,1)S(1)}, bf16[1,384,1280]{2,1,0:T(8,128)(2,1)S(1)}, bf16[1,384,1280]{2,1,0:T(8,128)(2,1)S(1)}, bf16[1,384,1280]{2,1,0:T(8,128)(2,1)S(1)}) custom-call(s32[8,5]{1,0:T(8,128)} %lists_hbm.1, bf16[1,384,1280]{2,1,0:T(8,128)(2,1)} %q_hbm.1, bf16[1,384,1280]{2,1,0:T(8,128)(2,1)} %k_hbm.1, bf16[1,384,1280]{2,1,0:T(8,128)(2,1)} %v_hbm.1, ...), custom_call_target="tpu_custom_call" | custom-call | tf_op jit(solution)/shard_map/tiles/pallas_call | solution.py:239
  178.2 2.0 %store.1 = (bf16[1,384,1280]{2,1,0:T(8,128)(2,1)}, bf16[1,384,1280]{2,1,0:T(8,128)(2,1)}, bf16[1,384,1280]{2,1,0:T(8,128)(2,1)}, bf16[1,384,1280]{2,1,0:T(8,128)(2,1)}) custom-call(bf16[1,384,1280]{2,1,0:T(8,128)(2,1)S(1)} %get-tuple-element.8.refs_0_, bf16[1,384,1280]{2,1,0:T(8,128)(2,1)S(1)} %get-tuple-element.9.refs_1_, ...), custom_call_target="tpu_custom_call" | custom-call | tf_op jit(solution)/shard_map/store/pallas_call | solution.py:263

commit v3 on v2

--- a/solution.py
+++ b/solution.py
@@ -209,7 +209,7 @@
 
 def store(*refs):
     sems = refs[8]
-    rows = refs[0].shape[1] // 2
+    rows = refs[0].shape[1] // 6
     copies = [
         pltpu.make_async_copy(
             refs[i].at[:, pl.ds(part * rows, rows)],
@@ -217,7 +217,7 @@
             sems.at[i, part],
         )
         for i in range(4)
-        for part in range(2)
+        for part in range(6)
     ]
     for copy in copies:
         copy.start()
@@ -265,7 +265,7 @@
         out_shape=(jax.ShapeDtypeStruct(queries.shape, jnp.bfloat16),) * 4,
         in_specs=[vmem] * 4,
         out_specs=(hbm,) * 4,
-        scratch_shapes=[dma((4, 2))],
+        scratch_shapes=[dma((4, 6))],
         compiler_params=pltpu.CompilerParams(vmem_limit_bytes=8 * 2**20),
         name="store",
     )(*[pltpu.with_memory_space_constraint(r, pltpu.VMEM) for r in results])

time: 180 us -> 180 us (level)
  no operation moved by 1% of the time
where the time goes in v3:
time: 180 us
  Pallas kernels  180 us (100%)
    pallas_call x1, Pallas kernels, on_device(): pl.pallas_call(functools.partial(kernel, grid_w), out_shape=(out,) * 4, i...  178 us

profile of v3, /device:TPU:0, one launch (start us, length us, event | category | flops | bytes accessed | tf_op | source)
XLA Modules:
  0.0 180.3 jit_solution(4864629777734392229)
XLA Ops:
  0.6 177.6 %tiles.1 = (bf16[1,384,1280]{2,1,0:T(8,128)(2,1)S(1)}, bf16[1,384,1280]{2,1,0:T(8,128)(2,1)S(1)}, bf16[1,384,1280]{2,1,0:T(8,128)(2,1)S(1)}, bf16[1,384,1280]{2,1,0:T(8,128)(2,1)S(1)}) custom-call(s32[8,5]{1,0:T(8,128)} %lists_hbm.1, bf16[1,384,1280]{2,1,0:T(8,128)(2,1)} %q_hbm.1, bf16[1,384,1280]{2,1,0:T(8,128)(2,1)} %k_hbm.1, bf16[1,384,1280]{2,1,0:T(8,128)(2,1)} %v_hbm.1, ...), custom_call_target="tpu_custom_call" | custom-call | tf_op jit(solution)/shard_map/tiles/pallas_call | solution.py:239
  178.2 2.1 %store.1 = (bf16[1,384,1280]{2,1,0:T(8,128)(2,1)}, bf16[1,384,1280]{2,1,0:T(8,128)(2,1)}, bf16[1,384,1280]{2,1,0:T(8,128)(2,1)}, bf16[1,384,1280]{2,1,0:T(8,128)(2,1)}) custom-call(bf16[1,384,1280]{2,1,0:T(8,128)(2,1)S(1)} %get-tuple-element.8.refs_0_, bf16[1,384,1280]{2,1,0:T(8,128)(2,1)S(1)} %get-tuple-element.9.refs_1_, ...), custom_call_target="tpu_custom_call" | custom-call | tf_op jit(solution)/shard_map/store/pallas_call | solution.py:263
